TPU v7x, 256 devices: a whole 4x4x8 slice. The times are simulated.
256 devices in a mesh: gx: 16 (over x_lo, z), gz: 16 (over y, x_hi, core).
Axes of the slice: x: 4 (x_hi: 2, x_lo: 2; x = x_hi * 2 + x_lo), y: 4, z: 8, core: 2. Of those that a mesh axis runs over, the one named last changes fastest.
Arguments:
- conserved_fields: float32 [6, 256, 512, 128], P(None, 'gx', 'gz'), may hold values from -2 to 62, as said below
- coeff: bfloat16 [2, 1024, 6, 128, 512], P(None, 'gx', None, 'gz'), may hold values from -0.25 to 0.25
- feed_plane: int32 [25], replicated, may hold values from 0 to 2047
Outputs:
- new_state: float32 [6, 256, 512, 128], P(None, 'gx', 'gz')
Inputs may be any that keep to these rules, and one draw needn't show every extreme that they name: `conserved_fields`: each cell is the conserved form of a gas with density 0.5 to 2, temperature 0.5 to 2, streamwise velocity -1 to 7, wall-normal and spanwise velocities -1 to 1 and vibrational energy per unit mass 0.05 to 0.5.
All inputs are finite; a program needn't handle non-finite values.
Results may differ from a plain program's by a relative error of at most 0.00038.
Values sent between devices are 32-bit elements; how exact they have to be, the bound alone decides.
A program may use at most 192 MiB of HBM per device.

v0:
```python
import math
import jax
import jax.numpy as jnp
from jax import lax
from jax.sharding import PartitionSpec as P

ADIABATIC_INDEX = 1.4
CAPACITY_CONST = 2.5
OSCILLATOR_SCALE = 2.0
VIBRANT_LAG = 0.5
LANDAU_FIT_LAW = 1.5
SURFACE_DIST_SQ = 0.36
TIME_STEP = 0.05
FORCING_RATE = 2.0
WENO_EPSILON = 1e-06


def cut_along(x, dim, devices):
    before, after = (x.shape[:dim], x.shape[dim + 1 :])
    return jnp.moveaxis(x.reshape(*before, devices, -1, *after), dim, 0)


def summed_on_arrival(x, axis, dim):
    devices = lax.axis_size(axis)
    tiles = lax.all_to_all(cut_along(x, dim, devices), axis, 0, 0, tiled=True)
    return jnp.sum(tiles, axis=0)


def with_halo(x, sides, width):
    for axis, dim in sides:
        devices, length = (lax.axis_size(axis), x.shape[dim])
        up = [(i, (i + 1) % devices) for i in range(devices)]
        down = [(j, i) for i, j in up]
        last = lax.slice_in_dim(x, length - width, length, axis=dim)
        leading = lax.slice_in_dim(x, 0, width, axis=dim)
        before = lax.ppermute(last, axis, up)
        after = lax.ppermute(leading, axis, down)
        x = jnp.concatenate([before, x, after], axis=dim)
    return x


def caloric_bundle(conserved_fields):
    fluid_rho_field = conserved_fields[0]
    motion_share = (
        0.5
        * (
            jnp.square(conserved_fields[1])
            + jnp.square(conserved_fields[2])
            + jnp.square(conserved_fields[3])
        )
        / jnp.square(fluid_rho_field)
    )
    translational_kelvin = (
        conserved_fields[4] / fluid_rho_field - motion_share - conserved_fields[5] / fluid_rho_field
    ) / CAPACITY_CONST
    thermodynamic_stress = fluid_rho_field * translational_kelvin
    return (fluid_rho_field, translational_kelvin, thermodynamic_stress)


def directional(extended_fields, component):
    fluid_rho_field, translational_kelvin, thermodynamic_stress = caloric_bundle(extended_fields)
    crossflow_flux_field = extended_fields[component] / fluid_rho_field
    flux_rows = []
    for member in range(6):
        entry = extended_fields[member] * crossflow_flux_field
        if member == component:
            entry = entry + thermodynamic_stress
        if member == 4:
            entry = entry + thermodynamic_stress * crossflow_flux_field
        flux_rows.append(entry)
    forcing_samples = jnp.abs(crossflow_flux_field) + jnp.sqrt(
        ADIABATIC_INDEX * translational_kelvin
    )
    return (jnp.stack(flux_rows), forcing_samples)


def weno_face(minus_two, minus_one, centre, plus_one, plus_two):
    low_poly = (2.0 * minus_two - 7.0 * minus_one + 11.0 * centre) / 6.0
    mid_poly = (-minus_one + 5.0 * centre + 2.0 * plus_one) / 6.0
    high_poly = (2.0 * centre + 5.0 * plus_one - plus_two) / 6.0
    low_beta = 13.0 / 12.0 * jnp.square(minus_two - 2.0 * minus_one + centre) + 0.25 * jnp.square(
        minus_two - 4.0 * minus_one + 3.0 * centre
    )
    mid_beta = 13.0 / 12.0 * jnp.square(minus_one - 2.0 * centre + plus_one) + 0.25 * jnp.square(
        minus_one - plus_one
    )
    high_beta = 13.0 / 12.0 * jnp.square(centre - 2.0 * plus_one + plus_two) + 0.25 * jnp.square(
        3.0 * centre - 4.0 * plus_one + plus_two
    )
    low_weight = 0.1 / jnp.square(WENO_EPSILON + low_beta)
    mid_weight = 0.6 / jnp.square(WENO_EPSILON + mid_beta)
    high_weight = 0.3 / jnp.square(WENO_EPSILON + high_beta)
    return (low_weight * low_poly + mid_weight * mid_poly + high_weight * high_poly) / (
        low_weight + mid_weight + high_weight
    )


def sweep_axis(extended_fields, axis, component):
    length = extended_fields.shape[axis] - 6
    fluxes, forcing_samples = directional(extended_fields, component)

    def window(array, offset, dim):
        return lax.slice_in_dim(array, offset, offset + length + 1, axis=dim)

    wave_speed = window(forcing_samples, 0, axis - 1)
    for offset in range(1, 6):
        wave_speed = jnp.maximum(wave_speed, window(forcing_samples, offset, axis - 1))
    wave_speed = wave_speed[None]
    upwind = [
        0.5 * (window(fluxes, offset, axis) + wave_speed * window(extended_fields, offset, axis))
        for offset in range(5)
    ]
    downwind = [
        0.5 * (window(fluxes, offset, axis) - wave_speed * window(extended_fields, offset, axis))
        for offset in (5, 4, 3, 2, 1)
    ]
    face_flux = weno_face(*upwind) + weno_face(*downwind)
    return lax.slice_in_dim(face_flux, 1, length + 1, axis=axis) - lax.slice_in_dim(
        face_flux, 0, length, axis=axis
    )


def wall_pad(conserved_fields):
    reflected_fields = conserved_fields[:, :, :, 2::-1]
    translational_kelvin = caloric_bundle(reflected_fields)[1]
    ghost_layer_kelvin = SURFACE_DIST_SQ / translational_kelvin
    ghost_layer_oscillator = reflected_fields[4] - CAPACITY_CONST * reflected_fields[0] * (
        translational_kelvin - ghost_layer_kelvin
    )
    ghost_cells = jnp.stack(
        [
            reflected_fields[0],
            -reflected_fields[1],
            -reflected_fields[2],
            -reflected_fields[3],
            ghost_layer_oscillator,
            reflected_fields[5],
        ]
    )
    top_cells = jnp.repeat(conserved_fields[:, :, :, -1:], 3, axis=3)
    return jnp.concatenate([ghost_cells, conserved_fields, top_cells], axis=3)


def relaxation(conserved_fields):
    fluid_rho_field, translational_kelvin, thermodynamic_stress = caloric_bundle(conserved_fields)
    balanced_oscillator_share = OSCILLATOR_SCALE / (
        jnp.exp(OSCILLATOR_SCALE / translational_kelvin) - 1.0
    )
    settling_interval = (
        VIBRANT_LAG
        * jnp.exp(LANDAU_FIT_LAW * (jnp.exp(-jnp.log(translational_kelvin) / 3.0) - 1.0))
        / thermodynamic_stress
    )
    return (fluid_rho_field * balanced_oscillator_share - conserved_fields[5]) / settling_interval


def local(conserved_fields, coeff, feed_plane):
    groups_x = lax.axis_size("gx")
    groups_z = lax.axis_size("gz")
    plane_count = conserved_fields.shape[1]
    span_cells = conserved_fields.shape[2]
    span_total = span_cells * groups_z
    kx_local = coeff.shape[1]
    levels_local = coeff.shape[3]
    span_modes = coeff.shape[4]
    stream_points = 2 * kx_local * groups_x
    planes = feed_plane.shape[0]
    span_ids = (
        jnp.arange(span_modes, dtype=jnp.int32)[:, None]
        * jnp.arange(span_total, dtype=jnp.int32)[None, :]
        % span_modes
    )
    span_angle = 2.0 * math.pi / span_modes * span_ids.astype(jnp.float32)
    span_table = jnp.concatenate([jnp.cos(span_angle), jnp.sin(span_angle)], axis=1).astype(
        jnp.bfloat16
    )
    mode_ids = lax.axis_index("gx") * kx_local + jnp.arange(kx_local, dtype=jnp.int32)
    stream_ids = feed_plane[:, None] * mode_ids[None, :] % stream_points
    stream_angle = 2.0 * math.pi / stream_points * stream_ids.astype(jnp.float32)
    stream_table = jnp.concatenate([jnp.cos(stream_angle), -jnp.sin(stream_angle)], axis=1).astype(
        jnp.bfloat16
    )
    coeff_rows = coeff.reshape(2 * kx_local * 6 * levels_local, span_modes)
    product = jnp.dot(coeff_rows, span_table, preferred_element_type=jnp.float32)
    product = product.reshape(2, kx_local, 6, levels_local, 2 * span_total)
    real_part = product[0, :, :, :, :span_total] - product[1, :, :, :, span_total:]
    imag_part = product[0, :, :, :, span_total:] + product[1, :, :, :, :span_total]
    mixed_modes = jnp.concatenate([real_part, imag_part], axis=0).astype(jnp.bfloat16)
    row_block = (6 * planes + groups_x - 1) // groups_x
    total_rows = row_block * groups_x
    table_rows = total_rows // 6 + 3
    padded_table = jnp.concatenate(
        [stream_table, jnp.zeros((table_rows - planes, 2 * kx_local), jnp.bfloat16)], axis=0
    )
    modes_flat = mixed_modes.reshape(2 * kx_local, 6 * levels_local * span_total)
    start = jnp.int32(0)
    plane_span = row_block * lax.axis_size("gx") // 6 + 2
    first_plane = start // 6
    table_block = lax.dynamic_slice_in_dim(padded_table, first_plane, plane_span, 0)
    products = jnp.dot(table_block, modes_flat, preferred_element_type=jnp.float32)
    products = products.reshape(plane_span * 6, levels_local * span_total)
    reduced = summed_on_arrival(
        lax.dynamic_slice_in_dim(products, start, row_block * lax.axis_size("gx"), 0), "gx", 0
    )
    reduced = reduced.reshape(row_block, levels_local, span_total)
    relaid = lax.all_to_all(reduced, "gz", split_axis=2, concat_axis=1, tiled=True)
    collected = lax.all_gather(relaid, "gx", axis=0, tiled=True)
    feed_values = collected[: 6 * planes].reshape(planes, 6, levels_local * groups_z, span_cells)
    target = jnp.transpose(feed_values, (1, 0, 3, 2))
    stream_pad = with_halo(conserved_fields, (("gx", 1),), 3)
    span_pad = with_halo(conserved_fields, (("gz", 2),), 3)
    at_inlet = lax.axis_index("gx") == 0
    at_outlet = lax.axis_index("gx") == groups_x - 1
    lower = jnp.where(at_inlet, jnp.repeat(conserved_fields[:, :1], 3, axis=1), stream_pad[:, :3])
    upper = jnp.where(
        at_outlet, jnp.repeat(conserved_fields[:, -1:], 3, axis=1), stream_pad[:, -3:]
    )
    stream_pad = jnp.concatenate([lower, conserved_fields, upper], axis=1)
    tendency = -(
        sweep_axis(stream_pad, 1, 1)
        + sweep_axis(span_pad, 2, 3)
        + sweep_axis(wall_pad(conserved_fields), 3, 2)
    )
    tendency = tendency.at[5].add(relaxation(conserved_fields))
    plane_global = lax.axis_index("gx") * plane_count + jnp.arange(plane_count, dtype=jnp.int32)
    inside = plane_global < planes
    strength = jnp.where(
        inside, FORCING_RATE * jnp.square(1.0 - plane_global.astype(jnp.float32) / planes), 0.0
    )
    picked = jnp.take(target, jnp.minimum(plane_global, planes - 1), axis=1)
    tendency = tendency + strength[None, :, None, None] * (picked - conserved_fields)
    return conserved_fields + TIME_STEP * tendency


def solution(mesh):
    placed = (P(None, "gx", "gz", None), P(None, "gx", None, "gz", None), P())
    return jax.shard_map(
        local, mesh=mesh, in_specs=placed, out_specs=P(None, "gx", "gz", None), check_vma=False
    )
```

profile of v0, /device:TPU:8, one launch (start us, length us, event | category | flops | bytes accessed | tf_op | source)
XLA Modules:
  0.0 323.3 jit_solution(15336654425104593148)
XLA Ops:
  9.0 2.3 collective-permute-start.3
  12.3 5.9 %collective-permute-start.1 = (f32[6,3,32,128]{3,2,0,1:T(8,128)}, f32[6,3,32,128]{3,2,0,1:T(8,128)}, u32[]{:S(2)}, u32[]{:S(2)}) collective-permute-start(f32[6,3,32,128]{3,2,0,1:T(8,128)} %get-tuple-element.31), channel_id=1, source_target_pairs={{16,0},{32,16},{48,32},{64,48},{80,64},{96,80},{112,96},{128,112},... | collective-permute-start | bytes 884744 | tf_op jit(solution)/shard_map/ppermute | solution.py:37
  18.2 4.9 %sine_convert_fusion = (bf16[512,512]{1,0:T(8,128)(2,1)}, bf16[512,512]{1,0:T(8,128)(2,1)}) fusion(), kind=kLoop, calls=%fused_computation.114 | loop fusion | flops 4194304 | bytes 1048576 | tf_op jit(solution)/shard_map/convert.5
  23.1 14.0 %convolution_bitcast_fusion = f32[6144,1024]{0,1:T(8,128)} fusion(bf16[6144,512]{1,0:T(8,128)(2,1)} %bitcast.56, bf16[512,512]{1,0:T(8,128)(2,1)} %get-tuple-element.44, bf16[512,512]{1,0:T(8,128)(2,1)} %get-tuple-element.45), kind=kOutput, calls=%fused_computation.1 | convolution fusion | flops 6444548096 | bytes 32505856 | tf_op jit(solution)/shard_map/dot_general | solution.py:184
  37.1 24.7 %copy.173 = f32[6144,1024]{1,0:T(8,128)} copy(f32[6144,1024]{0,1:T(8,128)} %convolution_bitcast_fusion) | data formatting | bytes 50331648 | tf_op jit(solution)/shard_map/dot_general | solution.py:184
  61.9 12.3 %fusion.1 = (bf16[1,64,6,8,512]{4,3,2,1,0:T(8,128)(2,1)}, bf16[1,64,6,8,512]{4,3,2,1,0:T(8,128)(2,1)}) fusion(f32[2,64,6,8,1024]{4,3,2,1,0:T(8,128)} %bitcast.47), kind=kLoop, calls=%fused_computation.5 | loop fusion | flops 6291456 | bytes 31457280 | tf_op jit(solution)/shard_map/convert.3
  74.1 4.8 %add.739 = bf16[64,24576]{1,0:T(8,128)(2,1)} reshape(bf16[1,64,6,8,512]{4,3,2,1,0:T(8,128)(2,1)} %get-tuple-element.27) | data formatting | bytes 6291456 | tf_op jit(solution)/shard_map/add | solution.py:187
  79.0 4.8 %sub.382 = bf16[64,24576]{1,0:T(8,128)(2,1)} reshape(bf16[1,64,6,8,512]{4,3,2,1,0:T(8,128)(2,1)} %get-tuple-element.26) | data formatting | bytes 6291456 | tf_op jit(solution)/shard_map/sub | solution.py:186
  84.0 5.6 %fusion.2 = f32[28,24576]{1,0:T(8,128)} fusion(bf16[64,24576]{1,0:T(8,128)(2,1)} %add.739, bf16[64,24576]{1,0:T(8,128)(2,1)} %sub.382, bf16[25,64]{1,0:T(8,128)(2,1)S(1)} %get-tuple-element.43, bf16[25,64]{1,0:T(8,128)(2,1)S(1)} %get-tuple-element.42), kind=kOutput, calls=%fused_computation.6 | convolution fusion | flops 188772352 | bytes 9050368 | tf_op jit(solution)/shard_map/dot_general | solution.py:200
  89.5 3.3 %reshape.160 = f32[168,4096]{1,0:T(8,128)} reshape(f32[28,24576]{1,0:T(8,128)} %fusion.2) | data formatting | bytes 5505024 | tf_op jit(solution)/shard_map/reshape | solution.py:201
  92.8 3.5 %dynamic_slice.8 = f32[160,4096]{1,0:T(8,128)} slice(f32[168,4096]{1,0:T(8,128)} %reshape.160), slice={[0:160], [0:4096]} | slice | bytes 5242880 | tf_op jit(solution)/shard_map/dynamic_slice | solution.py:203
  96.3 3.5 %reshape.161 = f32[16,10,4096]{2,1,0:T(8,128)} reshape(f32[160,4096]{1,0:T(8,128)} %dynamic_slice.8) | data formatting | bytes 5242880 | tf_op jit(solution)/shard_map/reshape | solution.py:20
  99.8 5.6 %all-to-all-start = ((f32[16,10,4096]{2,1,0:T(8,128)}), f32[16,10,4096]{2,1,0:T(8,128)}, u32[]{:S(2)}, u32[]{:S(2)}) async-start(f32[16,10,4096]{2,1,0:T(8,128)} %reshape.161), calls=%async_computation | async-start | bytes 8388608 | tf_op jit(solution)/shard_map/all_to_all | solution.py:25
  105.4 3.1 slice.508
  110.4 2.8 copy.191
  131.8 2.7 copy.162
  139.4 19.7 %divide_add_fusion = f32[6,16,32,129]{3,2,0,1:T(8,128)} fusion(f32[6,16,32,3]{3,2,0,1:T(8,128)S(1)} %reshape.157, f32[6,16,32,128]{3,2,0,1:T(8,128)S(1)} %get-tuple-element.35, f32[6,16,32,134]{3,2,0,1:T(8,128)S(1)} %multiply_dynamic-update-slice_fusion.1, f32[6,16,32,3]{3,2,0,1:T(8,128)S(1)} %copy-done.4, f32[16,32,129]{2,1,0:T(8,128)S(1)} %slice_maximum_fusion), kind=kLoop, calls=%fused_computation.33 | loop fusion | flops 60632064 | bytes 13006848 | tf_op jit(solution)/shard_map/add | solution.py:117
  162.2 13.0 %divide_add_fusion.1 = f32[6,16,33,128]{3,2,0,1:T(8,128)} fusion(f32[6,16,35,128]{3,2,0,1:T(8,128)S(1)} %constant_dynamic-update-slice_fusion, f32[6,16,38,128]{3,2,0,1:T(8,128)S(1)} %multiply_dynamic-update-slice_fusion.11, f32[6,16,32,128]{3,2,0,1:T(8,128)S(1)} %get-tuple-element.35, f32[6,16,3,128]{3,2,0,1:T(4,128)} %collective-permute-done.2, ...), kind=kLoop, calls=%fused_computation.62 | loop fusion | flops 60825600 | bytes 18210816 | tf_op jit(solution)/shard_map/add | solution.py:117
  179.5 22.3 %all-to-all-done = f32[16,10,4096]{2,1,0:T(8,128)} async-done(((f32[16,10,4096]{2,1,0:T(8,128)}), f32[16,10,4096]{2,1,0:T(8,128)}, u32[]{:S(2)}, u32[]{:S(2)}) %all-to-all-start) | async-done | bytes 2621472 | tf_op jit(solution)/shard_map/all_to_all | solution.py:25
  201.9 2.4 reduce_sum.9
  204.5 2.0 copy.174
  206.6 4.0 %reshape.206 = f32[16,1,2560]{2,1,0:T(1,128)} reshape(f32[512,8,10]{2,1,0:T(8,128)} %bitcast.49) | data formatting | bytes 327680
  210.6 6.0 %all-to-all-start.1 = ((f32[16,1,2560]{2,1,0:T(1,128)}), f32[16,1,2560]{2,1,0:T(1,128)S(1)}, u32[]{:S(2)}, u32[]{:S(2)}) async-start(f32[16,1,2560]{2,1,0:T(1,128)} %reshape.206), calls=%async_computation.1 | async-start | bytes 327680 | tf_op jit(solution)/shard_map/all_to_all | solution.py:206
  217.4 5.6 %all-to-all-done.1 = f32[16,1,2560]{2,1,0:T(1,128)S(1)} async-done(((f32[16,1,2560]{2,1,0:T(1,128)}), f32[16,1,2560]{2,1,0:T(1,128)S(1)}, u32[]{:S(2)}, u32[]{:S(2)}) %all-to-all-start.1) | async-done | bytes 163872 | tf_op jit(solution)/shard_map/all_to_all | solution.py:206
  224.6 3.6 %reshape.207 = f32[512,8,10]{2,1,0:T(8,128)} reshape(f32[16,2560]{1,0:T(8,128)S(1)} %reduce.2) | data formatting | bytes 327680
  228.1 3.3 %copy.176 = f32[10,16,8,32]{3,2,1,0:T(8,128)} copy(f32[10,16,8,32]{0,2,3,1:T(8,128)} %bitcast.50) | data formatting | bytes 327680 | tf_op jit(solution)/shard_map/all_to_all | solution.py:206
  233.5 2.2 add_dynamic-update-slice_fusion.1
  240.0 11.2 %divide_add_fusion.2 = f32[6,17,32,128]{3,2,0,1:T(8,128)S(1)} fusion(f32[6,3,32,128]{3,2,0,1:T(8,128)S(1)} %broadcast_select_fusion, f32[6,16,32,128]{3,2,0,1:T(8,128)S(1)} %get-tuple-element.35, f32[6,22,32,128]{3,2,0,1:T(8,128)} %multiply_dynamic-update-slice_fusion.6, f32[6,3,32,128]{3,2,0,1:T(8,128)S(1)} %copy-done.8, f32[17,32,128]{2,1,0:T(8,128)S(1)} %copy-done.9), kind=kLoop, calls=%fused_computation.87 | loop fusion | flops 63922176 | bytes 14139392 | tf_op jit(solution)/shard_map/add | solution.py:117
  253.2 2.0 fusion.70
  255.2 50.4 %all-gather.2.cloned.1.call-done = f32[160,128,32]{1,2,0:T(8,128)} async-done(((f32[10,128,32]{1,2,0:T(8,128)}), f32[160,128,32]{1,2,0:T(8,128)}) %all-gather.2.cloned.1.call-update) | async-done | bytes 2621456 | tf_op jit(solution)/shard_map/all_gather | solution.py:207
  309.0 3.6 %gather_fusion = f32[16,6,32,128]{3,2,1,0:T(8,128)} fusion(f32[6,25,32,128]{3,2,1,0:T(8,128)} %bitcast.51, s32[1024]{0:T(1024)S(1)} %pad_clamp_fusion), kind=kCustom, calls=%fused_computation | custom fusion | bytes 3145792 | tf_op jit(solution)/shard_map/jit(_take)/gather | solution.py:230
  312.6 2.5 fusion.52
  (97 shorter events, 51.6 us)
Async XLA Ops:
  9.0 150.0 %collective-permute-start.3 = (f32[6,16,3,128]{3,2,0,1:T(4,128)}, f32[6,16,3,128]{3,2,0,1:T(4,128)}, u32[]{:S(2)}, u32[]{:S(2)}) collective-permute-start(f32[6,16,3,128]{3,2,0,1:T(4,128)} %get-tuple-element.33), channel_id=1, source_target_pairs={{1,0},{2,1},{3,2},{4,3},{5,4},{6,5},{7,6},{8,7},{9,8},{10,9},{11,1... | collective-permute-start | bytes 442376 | tf_op jit(solution)/shard_map/ppermute | solution.py:37
  11.4 147.7 %collective-permute-start.2 = (f32[6,16,3,128]{3,2,0,1:T(4,128)}, f32[6,16,3,128]{3,2,0,1:T(4,128)}, u32[]{:S(2)}, u32[]{:S(2)}) collective-permute-start(f32[6,16,3,128]{3,2,0,1:T(4,128)} %get-tuple-element.32), channel_id=1, source_target_pairs={{0,1},{1,2},{2,3},{3,4},{4,5},{5,6},{6,7},{7,8},{8,9},{9,10},{10,1... | collective-permute-start | bytes 442376 | tf_op jit(solution)/shard_map/ppermute | solution.py:36
  12.3 163.0 %collective-permute-start.1 = (f32[6,3,32,128]{3,2,0,1:T(8,128)}, f32[6,3,32,128]{3,2,0,1:T(8,128)}, u32[]{:S(2)}, u32[]{:S(2)}) collective-permute-start(f32[6,3,32,128]{3,2,0,1:T(8,128)} %get-tuple-element.31), channel_id=1, source_target_pairs={{16,0},{32,16},{48,32},{64,48},{80,64},{96,80},{112,96},{128,112},... | collective-permute-start | bytes 884744 | tf_op jit(solution)/shard_map/ppermute | solution.py:37
  18.2 158.1 %collective-permute-start = (f32[6,3,32,128]{3,2,0,1:T(8,128)}, f32[6,3,32,128]{3,2,0,1:T(8,128)}, u32[]{:S(2)}, u32[]{:S(2)}) collective-permute-start(f32[6,3,32,128]{3,2,0,1:T(8,128)} %get-tuple-element.30), channel_id=1, source_target_pairs={{0,16},{16,32},{32,48},{48,64},{64,80},{80,96},{96,112},{112,128},... | collective-permute-start | bytes 884744 | tf_op jit(solution)/shard_map/ppermute | solution.py:36
  79.0 4.8 %copy-start.12 = (s32[25]{0:T(128)S(1)}, s32[25]{0:T(128)}, u32[]{:S(2)}) copy-start(s32[25]{0:T(128)} %param.7) | copy-start | bytes 304
  99.8 102.1 %all-to-all-start = ((f32[16,10,4096]{2,1,0:T(8,128)}), f32[16,10,4096]{2,1,0:T(8,128)}, u32[]{:S(2)}, u32[]{:S(2)}) async-start(f32[16,10,4096]{2,1,0:T(8,128)} %reshape.161), calls=%async_computation | async-start | bytes 8388608 | tf_op jit(solution)/shard_map/all_to_all | solution.py:25
  105.4 3.2 copy-start
  134.5 1.4 copy-start.4
  162.2 13.0 %copy-start.11 = (f32[6,32,128]{2,1,0:T(8,128)S(1)}, f32[6,32,128]{2,1,0:T(8,128)}, u32[]{:S(2)}) copy-start(f32[6,32,128]{2,1,0:T(8,128)} %get-tuple-element.29) | copy-start | bytes 294916
  162.2 14.1 %copy-start.10 = (f32[6,32,128]{2,1,0:T(8,128)S(1)}, f32[6,32,128]{2,1,0:T(8,128)}, u32[]{:S(2)}) copy-start(f32[6,32,128]{2,1,0:T(8,128)} %get-tuple-element.28) | copy-start | bytes 294916
  176.3 0.7 copy-start.7
  177.3 1.4 copy-start.2
  210.6 12.4 %all-to-all-start.1 = ((f32[16,1,2560]{2,1,0:T(1,128)}), f32[16,1,2560]{2,1,0:T(1,128)S(1)}, u32[]{:S(2)}, u32[]{:S(2)}) async-start(f32[16,1,2560]{2,1,0:T(1,128)} %reshape.206), calls=%async_computation.1 | async-start | bytes 327680 | tf_op jit(solution)/shard_map/all_to_all | solution.py:206
  216.6 89.0 %all-gather.2.cloned.1.call-start = ((), (), s32[]{:S(2)}) async-start(), calls=%async_computation.2 | async-start | bytes 2785280 | tf_op jit(solution)/shard_map/all_gather | solution.py:207
  233.5 4.0 %copy-start.3 = (f32[6,22,32,128]{3,2,0,1:T(8,128)S(1)}, f32[6,22,32,128]{3,2,0,1:T(8,128)}, u32[]{:S(2)}) copy-start(f32[6,22,32,128]{3,2,0,1:T(8,128)} %copy-done.2) | copy-start | bytes 6488068
  237.4 2.6 copy-start.8
  237.4 2.6 copy-start.9
  240.0 11.3 %copy-start.5 = (f32[6,16,33,128]{3,2,0,1:T(8,128)S(1)}, f32[6,16,33,128]{3,2,0,1:T(8,128)}, u32[]{:S(2)}) copy-start(f32[6,16,33,128]{3,2,0,1:T(8,128)} %divide_add_fusion.1) | copy-start | bytes 4866052
  240.0 11.3 %copy-start.6 = (f32[6,16,32,129]{3,2,0,1:T(8,128)S(1)}, f32[6,16,32,129]{3,2,0,1:T(8,128)}, u32[]{:S(2)}) copy-start(f32[6,16,32,129]{3,2,0,1:T(8,128)} %divide_add_fusion) | copy-start | bytes 4755460
  305.6 1.7 slice-start
  309.0 3.6 %copy-start.1 = (f32[6,16,32,128]{3,2,1,0:T(8,128)S(1)}, f32[6,16,32,128]{3,2,1,0:T(8,128)}, u32[]{:S(2)}) copy-start(f32[6,16,32,128]{3,2,1,0:T(8,128)} %param.5) | copy-start | bytes 4718596
Sparse Core Ops, SparseCore 0:
  233.6 71.9 all-gather.1
where the time goes:
time: 325 us; the launch traced here: 323 us
  local copies, waits for them, and re-layouts  99.8 us (31%)
  other arithmetic  91.9 us (28%)
  waiting for transfers between devices  78.4 us (24%)
  starting transfers between devices  19.9 us (6%)
  matrix products  19.6 us (6%)
  between operations  13.7 us (4%)
    all_gather x1, waiting for transfers between devices, local(): collected = lax.all_gather(relaid, 'gx', axis=0, tiled=True)  50.4 us
    add x3, other arithmetic, sweep_axis(): face_flux = weno_face(*upwind) + weno_face(*downwind)  44 us
    dot_general x1, local copies, waits for them, and re-layouts, local(): jnp.dot(coeff_rows, span_table, preferred_element_type=jnp.float32)  24.7 us
    unnamed x37, local copies, waits for them, and re-layouts  23 us
    all_to_all x1, waiting for transfers between devices, summed_on_arrival(): tiles = lax.all_to_all(cut_along(x, dim, devices), axis, 0, 0, tiled=True)  22.3 us
    another operation x3, other arithmetic  17.4 us
    dot_general x1, matrix products, local(): jnp.dot(coeff_rows, span_table, preferred_element_type=jnp.float32)  14 us
    unnamed x19, other arithmetic  13 us
  transfers between devices with their start and end apart: 7, of which 3 were waited for; matrix products, arithmetic and copies ran while one was open for 55% of the time, Pallas kernels for 0%

commit v1 on v0

--- a/solution.py
+++ b/solution.py
@@ -204,7 +204,12 @@
     )
     reduced = reduced.reshape(row_block, levels_local, span_total)
     relaid = lax.all_to_all(reduced, "gz", split_axis=2, concat_axis=1, tiled=True)
-    collected = lax.all_gather(relaid, "gx", axis=0, tiled=True)
+    nodes = []
+    for _ in range(lax.axis_size("gx")):
+        nodes.append(relaid)
+    local_out = jnp.stack(nodes)
+    m_next = lax.all_to_all(local_out, "gx", 0, 0)
+    collected = jnp.concatenate(m_next, 0)
     feed_values = collected[: 6 * planes].reshape(planes, 6, levels_local * groups_z, span_cells)
     target = jnp.transpose(feed_values, (1, 0, 3, 2))
     stream_pad = with_halo(conserved_fields, (("gx", 1),), 3)

time: 325 us -> 313 us (0.963); the launches traced: 323 us -> 308 us
  between operations: 13.7 us -> 0.36 us
  waiting for transfers between devices: 78.4 us -> 66 us
  starting transfers between devices: 19.9 us -> 28 us
    all_gather x1 -> x0, waiting for transfers between devices: 50.4 us -> none  [local(): collected = lax.all_gather(relaid, 'gx', axis=0, tiled=True)]
    all_to_all x0 -> x1, waiting for transfers between devices: none -> 38.1 us  [local(): m_next = lax.all_to_all(local_out, 'gx', 0, 0)]
    all_to_all x0 -> x1, starting transfers between devices: none -> 8.2 us  [local(): m_next = lax.all_to_all(local_out, 'gx', 0, 0)]
  transfers between devices with their start and end apart: 7 -> 7, of which waited for: 3 -> 3; matrix products, arithmetic and copies ran while one was open for 55% -> 58% of each run, Pallas kernels for 0% -> 0%
where the time goes in v1:
time: 313 us; the launch traced here: 308 us
  local copies, waits for them, and re-layouts  101 us (32%)
  other arithmetic  92.3 us (29%)
  waiting for transfers between devices  66 us (21%)
  starting transfers between devices  28 us (9%)
  matrix products  19.6 us (6%)
    add x3, other arithmetic, sweep_axis(): face_flux = weno_face(*upwind) + weno_face(*downwind)  44.5 us
    all_to_all x1, waiting for transfers between devices, local(): m_next = lax.all_to_all(local_out, 'gx', 0, 0)  38.1 us
    dot_general x1, local copies, waits for them, and re-layouts, local(): jnp.dot(coeff_rows, span_table, preferred_element_type=jnp.float32)  24.8 us
    unnamed x37, local copies, waits for them, and re-layouts  23 us
    all_to_all x1, waiting for transfers between devices, summed_on_arrival(): tiles = lax.all_to_all(cut_along(x, dim, devices), axis, 0, 0, tiled=True)  22.3 us
    another operation x3, other arithmetic  17.3 us
    dot_general x1, matrix products, local(): jnp.dot(coeff_rows, span_table, preferred_element_type=jnp.float32)  14 us
    unnamed x19, other arithmetic  12.9 us
  transfers between devices with their start and end apart: 7, of which 3 were waited for; matrix products, arithmetic and copies ran while one was open for 58% of the time, Pallas kernels for 0%

profile of v1, /device:TPU:8, one launch (start us, length us, event | category | flops | bytes accessed | tf_op | source)
XLA Modules:
  0.0 307.7 jit_solution(5888211737631620050)
XLA Ops:
  2.5 2.3 collective-permute-start.3
  5.8 5.9 %collective-permute-start.1 = (f32[6,3,32,128]{3,2,0,1:T(8,128)}, f32[6,3,32,128]{3,2,0,1:T(8,128)}, u32[]{:S(2)}, u32[]{:S(2)}) collective-permute-start(f32[6,3,32,128]{3,2,0,1:T(8,128)} %get-tuple-element.31), channel_id=1, source_target_pairs={{16,0},{32,16},{48,32},{64,48},{80,64},{96,80},{112,96},{128,112},... | collective-permute-start | bytes 884744 | tf_op jit(solution)/shard_map/ppermute | solution.py:37
  11.7 4.9 %sine_convert_fusion = (bf16[512,512]{1,0:T(8,128)(2,1)}, bf16[512,512]{1,0:T(8,128)(2,1)}) fusion(), kind=kLoop, calls=%fused_computation.114 | loop fusion | flops 4194304 | bytes 1048576 | tf_op jit(solution)/shard_map/convert.5
  16.6 14.0 %convolution_bitcast_fusion = f32[6144,1024]{0,1:T(8,128)} fusion(bf16[6144,512]{1,0:T(8,128)(2,1)} %bitcast.56, bf16[512,512]{1,0:T(8,128)(2,1)} %get-tuple-element.44, bf16[512,512]{1,0:T(8,128)(2,1)} %get-tuple-element.45), kind=kOutput, calls=%fused_computation.1 | convolution fusion | flops 6444548096 | bytes 32505856 | tf_op jit(solution)/shard_map/dot_general | solution.py:184
  30.6 24.8 %copy.173 = f32[6144,1024]{1,0:T(8,128)} copy(f32[6144,1024]{0,1:T(8,128)} %convolution_bitcast_fusion) | data formatting | bytes 50331648 | tf_op jit(solution)/shard_map/dot_general | solution.py:184
  55.3 12.2 %fusion.1 = (bf16[1,64,6,8,512]{4,3,2,1,0:T(8,128)(2,1)}, bf16[1,64,6,8,512]{4,3,2,1,0:T(8,128)(2,1)}) fusion(f32[2,64,6,8,1024]{4,3,2,1,0:T(8,128)} %bitcast.47), kind=kLoop, calls=%fused_computation.5 | loop fusion | flops 6291456 | bytes 31457280 | tf_op jit(solution)/shard_map/convert.3
  67.6 4.8 %add.739 = bf16[64,24576]{1,0:T(8,128)(2,1)} reshape(bf16[1,64,6,8,512]{4,3,2,1,0:T(8,128)(2,1)} %get-tuple-element.27) | data formatting | bytes 6291456 | tf_op jit(solution)/shard_map/add | solution.py:187
  72.4 4.8 %sub.382 = bf16[64,24576]{1,0:T(8,128)(2,1)} reshape(bf16[1,64,6,8,512]{4,3,2,1,0:T(8,128)(2,1)} %get-tuple-element.26) | data formatting | bytes 6291456 | tf_op jit(solution)/shard_map/sub | solution.py:186
  77.4 5.6 %fusion.2 = f32[28,24576]{1,0:T(8,128)} fusion(bf16[64,24576]{1,0:T(8,128)(2,1)} %add.739, bf16[64,24576]{1,0:T(8,128)(2,1)} %sub.382, bf16[25,64]{1,0:T(8,128)(2,1)S(1)} %get-tuple-element.43, bf16[25,64]{1,0:T(8,128)(2,1)S(1)} %get-tuple-element.42), kind=kOutput, calls=%fused_computation.6 | convolution fusion | flops 188772352 | bytes 9050368 | tf_op jit(solution)/shard_map/dot_general | solution.py:200
  83.0 3.3 %reshape.166 = f32[168,4096]{1,0:T(8,128)} reshape(f32[28,24576]{1,0:T(8,128)} %fusion.2) | data formatting | bytes 5505024 | tf_op jit(solution)/shard_map/reshape | solution.py:201
  86.2 3.5 %dynamic_slice.8 = f32[160,4096]{1,0:T(8,128)} slice(f32[168,4096]{1,0:T(8,128)} %reshape.166), slice={[0:160], [0:4096]} | slice | bytes 5242880 | tf_op jit(solution)/shard_map/dynamic_slice | solution.py:203
  89.8 3.4 %reshape.167 = f32[16,10,4096]{2,1,0:T(8,128)} reshape(f32[160,4096]{1,0:T(8,128)} %dynamic_slice.8) | data formatting | bytes 5242880 | tf_op jit(solution)/shard_map/reshape | solution.py:20
  93.2 5.6 %all-to-all-start = ((f32[16,10,4096]{2,1,0:T(8,128)}), f32[16,10,4096]{2,1,0:T(8,128)}, u32[]{:S(2)}, u32[]{:S(2)}) async-start(f32[16,10,4096]{2,1,0:T(8,128)} %reshape.167), calls=%async_computation | async-start | bytes 8388608 | tf_op jit(solution)/shard_map/all_to_all | solution.py:25
  98.8 3.1 %slice.509 = f32[6,16,32,1]{3,2,1,0:T(8,128)} slice(f32[6,16,32,128]{3,2,1,0:T(8,128)} %param.5), slice={[0:6], [0:16], [0:32], [127:128]} | slice | bytes 24576 | tf_op jit(solution)/shard_map/slice | solution.py:140
  103.9 2.8 copy.191
  125.2 2.7 copy.162
  132.8 19.7 %divide_add_fusion = f32[6,16,32,129]{3,2,0,1:T(8,128)} fusion(f32[6,16,32,3]{3,2,0,1:T(8,128)S(1)} %reshape.163, f32[6,16,32,128]{3,2,0,1:T(8,128)S(1)} %get-tuple-element.35, f32[6,16,32,134]{3,2,0,1:T(8,128)S(1)} %multiply_dynamic-update-slice_fusion.1, f32[6,16,32,3]{3,2,0,1:T(8,128)S(1)} %copy-done.4, f32[16,32,129]{2,1,0:T(8,128)S(1)} %slice_maximum_fusion), kind=kLoop, calls=%fused_computation.33 | loop fusion | flops 60632064 | bytes 13006848 | tf_op jit(solution)/shard_map/add | solution.py:117
  155.6 13.1 %divide_add_fusion.1 = f32[6,16,33,128]{3,2,0,1:T(8,128)} fusion(f32[6,16,35,128]{3,2,0,1:T(8,128)S(1)} %constant_dynamic-update-slice_fusion, f32[6,16,38,128]{3,2,0,1:T(8,128)S(1)} %multiply_dynamic-update-slice_fusion.11, f32[6,16,32,128]{3,2,0,1:T(8,128)S(1)} %get-tuple-element.35, f32[6,16,3,128]{3,2,0,1:T(4,128)} %collective-permute-done.2, ...), kind=kLoop, calls=%fused_computation.62 | loop fusion | flops 60825600 | bytes 18210816 | tf_op jit(solution)/shard_map/add | solution.py:117
  173.0 22.3 %all-to-all-done = f32[16,10,4096]{2,1,0:T(8,128)} async-done(((f32[16,10,4096]{2,1,0:T(8,128)}), f32[16,10,4096]{2,1,0:T(8,128)}, u32[]{:S(2)}, u32[]{:S(2)}) %all-to-all-start) | async-done | bytes 2621472 | tf_op jit(solution)/shard_map/all_to_all | solution.py:25
  195.3 2.4 reduce_sum.9
  197.9 2.0 copy.174
  200.0 4.0 %reshape.212 = f32[16,1,2560]{2,1,0:T(1,128)} reshape(f32[512,8,10]{2,1,0:T(8,128)} %bitcast.49) | data formatting | bytes 327680
  204.0 6.0 %all-to-all-start.1 = ((f32[16,1,2560]{2,1,0:T(1,128)}), f32[16,1,2560]{2,1,0:T(1,128)S(1)}, u32[]{:S(2)}, u32[]{:S(2)}) async-start(f32[16,1,2560]{2,1,0:T(1,128)} %reshape.212), calls=%async_computation.1 | async-start | bytes 327680 | tf_op jit(solution)/shard_map/all_to_all | solution.py:206
  210.8 5.7 %all-to-all-done.1 = f32[16,1,2560]{2,1,0:T(1,128)S(1)} async-done(((f32[16,1,2560]{2,1,0:T(1,128)}), f32[16,1,2560]{2,1,0:T(1,128)S(1)}, u32[]{:S(2)}, u32[]{:S(2)}) %all-to-all-start.1) | async-done | bytes 163872 | tf_op jit(solution)/shard_map/all_to_all | solution.py:206
  218.0 3.6 %reshape.213 = f32[512,8,10]{2,1,0:T(8,128)} reshape(f32[16,2560]{1,0:T(8,128)S(1)} %reduce.2) | data formatting | bytes 327680
  221.5 3.3 %copy.176 = f32[10,16,8,32]{3,2,1,0:T(8,128)} copy(f32[10,16,8,32]{0,2,3,1:T(8,128)} %bitcast.50) | data formatting | bytes 327680 | tf_op jit(solution)/shard_map/all_to_all | solution.py:206
  228.1 8.2 %all-to-all-start.2 = ((f32[16,10,128,32]{2,3,1,0:T(8,128)}), f32[16,10,128,32]{2,3,1,0:T(8,128)}, u32[]{:S(2)}, u32[]{:S(2)}) async-start(f32[16,10,128,32]{2,3,1,0:T(8,128)} %stack.17), calls=%async_computation.2 | async-start | bytes 5242880 | tf_op jit(solution)/shard_map/all_to_all | solution.py:211
  236.3 2.2 add_dynamic-update-slice_fusion.1
  242.8 11.7 %divide_add_fusion.2 = f32[6,17,32,128]{3,2,0,1:T(8,128)S(1)} fusion(f32[6,3,32,128]{3,2,0,1:T(8,128)S(1)} %broadcast_select_fusion, f32[6,16,32,128]{3,2,0,1:T(8,128)S(1)} %get-tuple-element.35, f32[6,22,32,128]{3,2,0,1:T(8,128)} %multiply_dynamic-update-slice_fusion.6, f32[6,3,32,128]{3,2,0,1:T(8,128)S(1)} %copy-done.8, f32[17,32,128]{2,1,0:T(8,128)S(1)} %copy-done.9), kind=kLoop, calls=%fused_computation.87 | loop fusion | flops 63922176 | bytes 14139392 | tf_op jit(solution)/shard_map/add | solution.py:117
  258.5 38.1 %all-to-all-done.2 = f32[16,10,128,32]{2,3,1,0:T(8,128)} async-done(((f32[16,10,128,32]{2,3,1,0:T(8,128)}), f32[16,10,128,32]{2,3,1,0:T(8,128)}, u32[]{:S(2)}, u32[]{:S(2)}) %all-to-all-start.2) | async-done | bytes 2621472 | tf_op jit(solution)/shard_map/all_to_all | solution.py:211
  300.2 3.6 %gather_fusion = f32[16,6,32,128]{3,2,1,0:T(8,128)} fusion(f32[6,25,32,128]{3,2,1,0:T(8,128)} %bitcast.51, s32[1024]{0:T(1024)S(1)} %pad_clamp_fusion), kind=kCustom, calls=%fused_computation | custom fusion | bytes 3145792 | tf_op jit(solution)/shard_map/jit(_take)/gather | solution.py:235
  303.9 2.5 fusion.52
  (96 shorter events, 55.0 us)
Async XLA Ops:
  2.5 149.9 %collective-permute-start.3 = (f32[6,16,3,128]{3,2,0,1:T(4,128)}, f32[6,16,3,128]{3,2,0,1:T(4,128)}, u32[]{:S(2)}, u32[]{:S(2)}) collective-permute-start(f32[6,16,3,128]{3,2,0,1:T(4,128)} %get-tuple-element.33), channel_id=1, source_target_pairs={{1,0},{2,1},{3,2},{4,3},{5,4},{6,5},{7,6},{8,7},{9,8},{10,9},{11,1... | collective-permute-start | bytes 442376 | tf_op jit(solution)/shard_map/ppermute | solution.py:37
  4.9 147.6 %collective-permute-start.2 = (f32[6,16,3,128]{3,2,0,1:T(4,128)}, f32[6,16,3,128]{3,2,0,1:T(4,128)}, u32[]{:S(2)}, u32[]{:S(2)}) collective-permute-start(f32[6,16,3,128]{3,2,0,1:T(4,128)} %get-tuple-element.32), channel_id=1, source_target_pairs={{0,1},{1,2},{2,3},{3,4},{4,5},{5,6},{6,7},{7,8},{8,9},{9,10},{10,1... | collective-permute-start | bytes 442376 | tf_op jit(solution)/shard_map/ppermute | solution.py:36
  5.8 162.9 %collective-permute-start.1 = (f32[6,3,32,128]{3,2,0,1:T(8,128)}, f32[6,3,32,128]{3,2,0,1:T(8,128)}, u32[]{:S(2)}, u32[]{:S(2)}) collective-permute-start(f32[6,3,32,128]{3,2,0,1:T(8,128)} %get-tuple-element.31), channel_id=1, source_target_pairs={{16,0},{32,16},{48,32},{64,48},{80,64},{96,80},{112,96},{128,112},... | collective-permute-start | bytes 884744 | tf_op jit(solution)/shard_map/ppermute | solution.py:37
  11.7 158.1 %collective-permute-start = (f32[6,3,32,128]{3,2,0,1:T(8,128)}, f32[6,3,32,128]{3,2,0,1:T(8,128)}, u32[]{:S(2)}, u32[]{:S(2)}) collective-permute-start(f32[6,3,32,128]{3,2,0,1:T(8,128)} %get-tuple-element.30), channel_id=1, source_target_pairs={{0,16},{16,32},{32,48},{48,64},{64,80},{80,96},{96,112},{112,128},... | collective-permute-start | bytes 884744 | tf_op jit(solution)/shard_map/ppermute | solution.py:36
  72.4 4.8 %copy-start.12 = (s32[25]{0:T(128)S(1)}, s32[25]{0:T(128)}, u32[]{:S(2)}) copy-start(s32[25]{0:T(128)} %param.7) | copy-start | bytes 304
  93.2 102.1 %all-to-all-start = ((f32[16,10,4096]{2,1,0:T(8,128)}), f32[16,10,4096]{2,1,0:T(8,128)}, u32[]{:S(2)}, u32[]{:S(2)}) async-start(f32[16,10,4096]{2,1,0:T(8,128)} %reshape.167), calls=%async_computation | async-start | bytes 8388608 | tf_op jit(solution)/shard_map/all_to_all | solution.py:25
  98.8 3.2 %copy-start = (f32[6,16,32,128]{3,2,1,0:T(8,128)S(1)}, f32[6,16,32,128]{3,2,1,0:T(8,128)}, u32[]{:S(2)}) copy-start(f32[6,16,32,128]{3,2,1,0:T(8,128)} %param.5) | copy-start | bytes 4718596
  127.9 1.4 copy-start.4
  155.6 13.1 %copy-start.11 = (f32[6,32,128]{2,1,0:T(8,128)S(1)}, f32[6,32,128]{2,1,0:T(8,128)}, u32[]{:S(2)}) copy-start(f32[6,32,128]{2,1,0:T(8,128)} %get-tuple-element.29) | copy-start | bytes 294916
  155.6 14.1 %copy-start.10 = (f32[6,32,128]{2,1,0:T(8,128)S(1)}, f32[6,32,128]{2,1,0:T(8,128)}, u32[]{:S(2)}) copy-start(f32[6,32,128]{2,1,0:T(8,128)} %get-tuple-element.28) | copy-start | bytes 294916
  169.8 0.7 copy-start.7
  170.7 1.4 copy-start.2
  204.0 12.4 %all-to-all-start.1 = ((f32[16,1,2560]{2,1,0:T(1,128)}), f32[16,1,2560]{2,1,0:T(1,128)S(1)}, u32[]{:S(2)}, u32[]{:S(2)}) async-start(f32[16,1,2560]{2,1,0:T(1,128)} %reshape.212), calls=%async_computation.1 | async-start | bytes 327680 | tf_op jit(solution)/shard_map/all_to_all | solution.py:206
  228.1 68.5 %all-to-all-start.2 = ((f32[16,10,128,32]{2,3,1,0:T(8,128)}), f32[16,10,128,32]{2,3,1,0:T(8,128)}, u32[]{:S(2)}, u32[]{:S(2)}) async-start(f32[16,10,128,32]{2,3,1,0:T(8,128)} %stack.17), calls=%async_computation.2 | async-start | bytes 5242880 | tf_op jit(solution)/shard_map/all_to_all | solution.py:211
  236.3 4.0 %copy-start.3 = (f32[6,22,32,128]{3,2,0,1:T(8,128)S(1)}, f32[6,22,32,128]{3,2,0,1:T(8,128)}, u32[]{:S(2)}) copy-start(f32[6,22,32,128]{3,2,0,1:T(8,128)} %copy-done.2) | copy-start | bytes 6488068
  240.3 2.6 copy-start.8
  240.3 2.6 copy-start.9
  242.8 11.7 %copy-start.5 = (f32[6,16,33,128]{3,2,0,1:T(8,128)S(1)}, f32[6,16,33,128]{3,2,0,1:T(8,128)}, u32[]{:S(2)}) copy-start(f32[6,16,33,128]{3,2,0,1:T(8,128)} %divide_add_fusion.1) | copy-start | bytes 4866052
  242.8 11.8 %copy-start.6 = (f32[6,16,32,129]{3,2,0,1:T(8,128)S(1)}, f32[6,16,32,129]{3,2,0,1:T(8,128)}, u32[]{:S(2)}) copy-start(f32[6,16,32,129]{3,2,0,1:T(8,128)} %divide_add_fusion) | copy-start | bytes 4755460
  300.2 3.6 %copy-start.1 = (f32[6,16,32,128]{3,2,1,0:T(8,128)S(1)}, f32[6,16,32,128]{3,2,1,0:T(8,128)}, u32[]{:S(2)}) copy-start(f32[6,16,32,128]{3,2,1,0:T(8,128)} %param.5) | copy-start | bytes 4718596
